TPU v7x, 32 devices: a whole 2x2x4 slice. The times are simulated.
32 devices in a mesh: row: 8 (over y, x, core), col: 4 (over z).
Axes of the slice: x: 2, y: 2, z: 4, core: 2. Of those that a mesh axis runs over, the one named last changes fastest.
Arguments:
- tokens: bfloat16 [4, 4096, 1792], P(None, ('row', 'col')), may hold values from -12 to 12
- lengths: int32 [4, 8], replicated, may hold values from 1 to 1024, 4096 in all within a row
- permutation: int32 [4, 32], replicated, may hold values from 0 to 31, each once within a row
- cotangent: bfloat16 [4, 4096, 1792], P(None, ('row', 'col')), may hold values from -12 to 12
- norm1_gain: float32 [1792], replicated, may hold values from 0.5 to 1.5
- mixer_in: bfloat16 [1792, 1792], P('row', 'col'), may hold values from -0.125 to 0.125
- mixer_gate: bfloat16 [1792, 1792], P('row', 'col'), may hold values from -0.125 to 0.125
- conv_kernel: float32 [3, 1792], P(None, 'col'), may hold values from -2.5 to 2.5
- mixer_out: bfloat16 [1792, 1792], P('row', 'col'), may hold values from -0.125 to 0.125
- norm2_gain: float32 [1792], replicated, may hold values from 0.5 to 1.5
- ffn_gate: bfloat16 [1792, 4864], P('row', 'col'), may hold values from -0.125 to 0.125
- ffn_up: bfloat16 [1792, 4864], P('row', 'col'), may hold values from -0.125 to 0.125
- ffn_down: bfloat16 [1792, 4864], P('row', 'col'), may hold values from -0.078125 to 0.078125
Outputs:
- output: bfloat16 [4, 4096, 1792], P(None, ('row', 'col'))
- input_grad: float32 [4, 4096, 1792], P(None, ('row', 'col'))
- norm1_gain_grad: float32 [1792], P(('row', 'col'))
- mixer_in_grad: float32 [1792, 1792], P('row', 'col')
- mixer_gate_grad: float32 [1792, 1792], P('row', 'col')
- conv_kernel_grad: float32 [3, 1792], P(None, ('col', 'row'))
- mixer_out_grad: float32 [1792, 1792], P('row', 'col')
- norm2_gain_grad: float32 [1792], P(('row', 'col'))
- ffn_gate_grad: float32 [1792, 4864], P('row', 'col')
- ffn_up_grad: float32 [1792, 4864], P('row', 'col')
- ffn_down_grad: float32 [1792, 4864], P('row', 'col')
Inputs may be any that keep to these rules, and one draw needn't show every extreme that they name: Each row of lengths sums to 4096, and its largest entry is exactly 1024. `permutation`: each row holds every number of 0 to 31 once.
All inputs are finite; a program needn't handle non-finite values.
Results may differ from a plain program's by a relative error of at most 0.0083.
Values may be sent and summed in bfloat16 or wider, within the bound.
No kernel may reach another device: no remote copies, remote signals or barrier semaphores. Data moves between devices by JAX's collectives and lax.ppermute only.
A program may use at most 160 MiB of HBM per device.

v0:
```python
import jax
import jax.numpy as jnp
from jax import lax
from jax.sharding import PartitionSpec as P

BLOCK = 128
EPSILON = 1e-05


def contract_last(left, right):
    return lax.dot_general(
        left, right, (((1,), (1,)), ((), ())), preferred_element_type=jnp.float32
    )


def contract_first(left, right):
    return lax.dot_general(
        left, right, (((0,), (0,)), ((), ())), preferred_element_type=jnp.float32
    )


def spread(shard):
    return lax.all_gather(shard, "col", axis=0, tiled=True)


def spread_grad(shard):
    return lax.all_gather(shard, "col", axis=0, tiled=True)


def collect(partial_sum):
    return lax.psum_scatter(partial_sum, "col", scatter_dimension=0, tiled=True)


def collect_grad(partial_sum):
    return lax.psum_scatter(partial_sum, "col", scatter_dimension=0, tiled=True)


def per_device(
    tokens,
    lengths,
    permutation,
    cotangent,
    norm1_gain,
    mixer_in,
    mixer_gate,
    conv_kernel,
    mixer_out,
    norm2_gain,
    ffn_gate,
    ffn_up,
    ffn_down,
):
    micro_count, rows_local, full_width = tokens.shape
    group_rows = rows_local * lax.axis_size("col")
    block_size = BLOCK
    blocks_local = group_rows // block_size
    blocks_all = permutation.shape[1]
    row_index = lax.axis_index("row")
    width_local = conv_kernel.shape[1]
    within = jnp.arange(block_size, dtype=jnp.int32)
    blocks_range = jnp.arange(blocks_all, dtype=jnp.int32)
    outputs = []
    input_grads = []
    totals = None
    for micro_index in range(micro_count):
        gathered = (
            lax.all_gather(mixer_in, "row", axis=0, tiled=True),
            lax.all_gather(mixer_gate, "row", axis=0, tiled=True),
            lax.all_gather(ffn_gate, "row", axis=0, tiled=True),
            lax.all_gather(ffn_up, "row", axis=0, tiled=True),
            lax.all_gather(mixer_out, "row", axis=0, tiled=True),
            lax.all_gather(ffn_down, "row", axis=0, tiled=True),
        )
        w_in, w_gate, w_ffg, w_ffu, w_out, w_down = gathered
        local_in = tokens[micro_index].astype(jnp.float32)
        local_cot = cotangent[micro_index]
        dealt_order = permutation[micro_index]
        seq_len = lengths[micro_index]
        offsets = jnp.cumsum(seq_len) - seq_len
        own_blocks = lax.dynamic_slice_in_dim(dealt_order, row_index * blocks_local, blocks_local)
        inverse = jnp.sum(
            jnp.where(dealt_order[None, :] == blocks_range[:, None], blocks_range[None, :], 0),
            axis=1,
        )
        source = jnp.take(inverse, jnp.maximum(own_blocks - 1, 0))
        position = (own_blocks[:, None] * block_size + within[None, :]).reshape(-1)
        is_start = jnp.any(position[:, None] == offsets[None, :], axis=1)
        was_start = jnp.any(position[:, None] - 1 == offsets[None, :], axis=1)
        keep_one = jnp.where(is_start, 0.0, 1.0).astype(jnp.float32)[:, None]
        keep_two = jnp.where(is_start | was_start, 0.0, 1.0).astype(jnp.float32)[:, None]
        scale_one = lax.rsqrt(jnp.mean(local_in * local_in, axis=1, keepdims=True) + EPSILON)
        normed_one = local_in * scale_one
        hidden_one = spread((normed_one * norm1_gain).astype(jnp.bfloat16))
        signal = jnp.dot(hidden_one, w_in, preferred_element_type=jnp.float32)
        gating = jnp.dot(hidden_one, w_gate, preferred_element_type=jnp.float32)
        signal_blocks = signal.reshape(blocks_local, block_size, width_local)
        tails_all = lax.all_gather(signal_blocks[:, block_size - 2 :, :], "row", axis=0, tiled=True)
        before = jnp.take(tails_all, source, axis=0)
        extended = jnp.concatenate([before, signal_blocks], axis=1)
        shift_one = keep_one * extended[:, 1 : block_size + 1, :].reshape(group_rows, width_local)
        shift_two = keep_two * extended[:, 0:block_size, :].reshape(group_rows, width_local)
        mixed_sig = (
            conv_kernel[0] * signal + conv_kernel[1] * shift_one + conv_kernel[2] * shift_two
        )
        product = (mixed_sig * gating).astype(jnp.bfloat16)
        branch = collect(contract_last(product, w_out))
        residual = local_in + branch
        scale_two = lax.rsqrt(jnp.mean(residual * residual, axis=1, keepdims=True) + EPSILON)
        normed_two = residual * scale_two
        hidden_two = spread((normed_two * norm2_gain).astype(jnp.bfloat16))
        gate_val = jnp.dot(hidden_two, w_ffg, preferred_element_type=jnp.float32)
        up_val = jnp.dot(hidden_two, w_ffu, preferred_element_type=jnp.float32)
        sigmoid_gate = jax.nn.sigmoid(gate_val)
        activated = (gate_val * sigmoid_gate * up_val).astype(jnp.bfloat16)
        ffn_result = collect(contract_last(activated, w_down))
        outputs.append((residual + ffn_result).astype(jnp.bfloat16))
        grad_full = spread_grad(local_cot)
        grad_act = jnp.dot(grad_full, w_down, preferred_element_type=jnp.float32)
        grad_down = contract_first(grad_full, activated)
        silu_slope = sigmoid_gate * (1.0 + gate_val * (1.0 - sigmoid_gate))
        grad_gate = (grad_act * up_val * silu_slope).astype(jnp.bfloat16)
        grad_up = (grad_act * gate_val * sigmoid_gate).astype(jnp.bfloat16)
        grad_ffg = contract_first(hidden_two, grad_gate)
        grad_ffu = contract_first(hidden_two, grad_up)
        grad_hidden_two = collect_grad(
            contract_last(grad_gate, w_ffg) + contract_last(grad_up, w_ffu)
        )
        grad_gain_two = jnp.sum(grad_hidden_two * normed_two, axis=0)
        grad_norm_two = grad_hidden_two * norm2_gain
        inner_two = jnp.mean(grad_norm_two * normed_two, axis=1, keepdims=True)
        grad_residual = local_cot.astype(jnp.float32) + scale_two * (
            grad_norm_two - normed_two * inner_two
        )
        grad_branch = spread_grad(grad_residual.astype(jnp.bfloat16))
        grad_product = jnp.dot(grad_branch, w_out, preferred_element_type=jnp.float32)
        grad_out_w = contract_first(grad_branch, product)
        grad_mixed = grad_product * gating
        grad_gating = (grad_product * mixed_sig).astype(jnp.bfloat16)
        grad_kernel = jnp.stack(
            [
                jnp.sum(grad_mixed * signal, axis=0),
                jnp.sum(grad_mixed * shift_one, axis=0),
                jnp.sum(grad_mixed * shift_two, axis=0),
            ]
        )
        into_one = (conv_kernel[1] * keep_one * grad_mixed).reshape(
            blocks_local, block_size, width_local
        )
        into_two = (conv_kernel[2] * keep_two * grad_mixed).reshape(
            blocks_local, block_size, width_local
        )
        grad_extended = jnp.pad(into_one, ((0, 0), (1, 1), (0, 0))) + jnp.pad(
            into_two, ((0, 0), (0, 2), (0, 0))
        )
        grad_before = grad_extended[:, :2, :]
        grad_blocks = grad_extended[:, 2:, :] + (conv_kernel[0] * grad_mixed).reshape(
            blocks_local, block_size, width_local
        )
        chooser = (source[:, None] == blocks_range[None, :]).astype(jnp.float32)
        tail_terms = jnp.einsum("jn,jtd->ntd", chooser, grad_before)
        returned = lax.psum_scatter(
            tail_terms.astype(jnp.bfloat16), "row", scatter_dimension=0, tiled=True
        ).astype(jnp.float32)
        grad_blocks = jnp.concatenate(
            [grad_blocks[:, : block_size - 2, :], grad_blocks[:, block_size - 2 :, :] + returned],
            axis=1,
        )
        grad_signal = grad_blocks.reshape(group_rows, width_local).astype(jnp.bfloat16)
        grad_in_w = contract_first(hidden_one, grad_signal)
        grad_gate_w = contract_first(hidden_one, grad_gating)
        grad_hidden_one = collect_grad(
            contract_last(grad_signal, w_in) + contract_last(grad_gating, w_gate)
        )
        grad_gain_one = jnp.sum(grad_hidden_one * normed_one, axis=0)
        grad_norm_one = grad_hidden_one * norm1_gain
        inner_one = jnp.mean(grad_norm_one * normed_one, axis=1, keepdims=True)
        input_grads.append(grad_residual + scale_one * (grad_norm_one - normed_one * inner_one))
        partials = (
            grad_gain_one,
            grad_in_w,
            grad_gate_w,
            grad_kernel,
            grad_out_w,
            grad_gain_two,
            grad_ffg,
            grad_ffu,
            grad_down,
        )
        partials = (
            lax.psum_scatter(partials[0], "row", scatter_dimension=0, tiled=True),
            lax.psum_scatter(partials[1], "row", scatter_dimension=0, tiled=True),
            lax.psum_scatter(partials[2], "row", scatter_dimension=0, tiled=True),
            lax.psum_scatter(partials[3], "row", scatter_dimension=1, tiled=True),
            lax.psum_scatter(partials[4], "row", scatter_dimension=0, tiled=True),
            lax.psum_scatter(partials[5], "row", scatter_dimension=0, tiled=True),
            lax.psum_scatter(partials[6], "row", scatter_dimension=0, tiled=True),
            lax.psum_scatter(partials[7], "row", scatter_dimension=0, tiled=True),
            lax.psum_scatter(partials[8], "row", scatter_dimension=0, tiled=True),
        )
        if totals is None:
            totals = tuple(partials)
        else:
            totals = tuple((left_val + right_val for left_val, right_val in zip(totals, partials)))
    gain_one_total, gain_two_total = (
        lax.psum_scatter(totals[0], "col", scatter_dimension=0, tiled=True),
        lax.psum_scatter(totals[5], "col", scatter_dimension=0, tiled=True),
    )
    return (
        jnp.stack(outputs),
        jnp.stack(input_grads),
        gain_one_total,
        totals[1],
        totals[2],
        totals[3],
        totals[4],
        gain_two_total,
        totals[6],
        totals[7],
        totals[8],
    )


def solution(mesh):
    placed = (
        P(None, ("row", "col"), None),
        P(),
        P(),
        P(None, ("row", "col"), None),
        P(),
        P("row", "col"),
        P("row", "col"),
        P(None, "col"),
        P("row", "col"),
        P(),
        P("row", "col"),
        P("row", "col"),
        P("row", "col"),
    )
    return jax.shard_map(
        per_device,
        mesh=mesh,
        in_specs=placed,
        out_specs=(
            P(None, ("row", "col"), None),
            P(None, ("row", "col"), None),
            P(("row", "col")),
            P("row", "col"),
            P("row", "col"),
            P(None, ("col", "row")),
            P("row", "col"),
            P(("row", "col")),
            P("row", "col"),
            P("row", "col"),
            P("row", "col"),
        ),
        check_vma=False,
    )
```

profile of v0, /device:TPU:0, one launch (start us, length us, event | category | flops | bytes accessed | tf_op | source)
XLA Modules:
  0.0 2552.2 jit_solution(138353777836643099)
XLA Ops:
  18.1 37.2 %all-gather.27.cloned.1.call-done = bf16[512,1792]{1,0:T(8,128)(2,1)} async-done(((bf16[128,1792]{1,0:T(8,128)(2,1)}), bf16[512,1792]{1,0:T(8,128)(2,1)}) %all-gather.27.cloned.1.call-update) | async-done | bytes 1835024 | tf_op jit(solution)/shard_map/all_gather | solution.py:23
  55.2 27.6 %all-gather.29.cloned.1.call-done = bf16[1792,448]{1,0:T(8,128)(2,1)} async-done(((bf16[224,448]{1,0:T(8,128)(2,1)}), bf16[1792,448]{1,0:T(8,128)(2,1)}) %all-gather.29.cloned.1.call-update) | async-done | bytes 1605648 | tf_op jit(solution)/shard_map/all_gather | solution.py:67
  91.4 9.2 all_gather.98
  102.5 23.9 all-gather.43.cloned.1.call-done
  134.3 9.4 all_gather.106
  163.2 19.6 all-gather.33.cloned.1.call-done
  190.1 36.1 %all-gather.47.cloned.1.call-done = bf16[512,1792]{1,0:T(8,128)(2,1)} async-done(((bf16[128,1792]{1,0:T(8,128)(2,1)}), bf16[512,1792]{1,0:T(8,128)(2,1)}) %all-gather.47.cloned.1.call-update) | async-done | bytes 1835024 | tf_op jit(solution)/shard_map/all_gather | solution.py:23
  234.8 9.4 all_gather.109
  246.1 22.0 all-gather.51.cloned.1.call-done
  278.8 9.1 all_gather.112
  313.7 24.5 reduce-scatter.30.cloned.1.call-done
  338.3 71.1 %reduce-scatter.38.cloned.1.call-done = f32[128,1792]{1,0:T(8,128)} async-done(((f32[512,1792]{1,0:T(8,128)}), f32[128,1792]{1,0:T(8,128)}) %reduce-scatter.38.cloned.1.call-update) | async-done | bytes 917520 | tf_op jit(solution)/shard_map/reduce_scatter | solution.py:31
  409.4 71.0 %reduce-scatter.42.cloned.1.call-done = f32[128,1792]{1,0:T(8,128)} async-done(((f32[512,1792]{1,0:T(8,128)}), f32[128,1792]{1,0:T(8,128)}) %reduce-scatter.42.cloned.1.call-update) | async-done | bytes 917520 | tf_op jit(solution)/shard_map/reduce_scatter | solution.py:31
  480.4 71.1 %reduce-scatter.34.cloned.1.call-done = f32[128,1792]{1,0:T(8,128)} async-done(((f32[512,1792]{1,0:T(8,128)}), f32[128,1792]{1,0:T(8,128)}) %reduce-scatter.34.cloned.1.call-update) | async-done | bytes 917520 | tf_op jit(solution)/shard_map/reduce_scatter | solution.py:31
  563.6 28.5 %all-gather.37.cloned.1.call-done = bf16[1792,1216]{1,0:T(8,128)(2,1)} async-done(((bf16[224,1216]{1,0:T(8,128)(2,1)}), bf16[1792,1216]{1,0:T(8,128)(2,1)}) %all-gather.37.cloned.1.call-update) | async-done | bytes 4358160 | tf_op jit(solution)/shard_map/all_gather | solution.py:69
  592.0 43.6 %all-gather.49.cloned.1.call-done = bf16[512,1792]{1,0:T(8,128)(2,1)} async-done(((bf16[128,1792]{1,0:T(8,128)(2,1)}), bf16[512,1792]{1,0:T(8,128)(2,1)}) %all-gather.49.cloned.1.call-update) | async-done | bytes 1835024 | tf_op jit(solution)/shard_map/all_gather | solution.py:23
  642.4 32.2 %all-gather.39.cloned.1.call-done = bf16[1792,1216]{1,0:T(8,128)(2,1)} async-done(((bf16[224,1216]{1,0:T(8,128)(2,1)}), bf16[1792,1216]{1,0:T(8,128)(2,1)}) %all-gather.39.cloned.1.call-update) | async-done | bytes 4358160 | tf_op jit(solution)/shard_map/all_gather | solution.py:70
  674.6 6.8 fusion.149
  681.4 36.1 %all-gather.67.cloned.1.call-done = bf16[1,512,1792]{2,1,0:T(8,128)(2,1)} async-done(((bf16[1,128,1792]{2,1,0:T(8,128)(2,1)}), bf16[1,512,1792]{2,1,0:T(8,128)(2,1)}) %all-gather.67.cloned.1.call-update) | async-done | bytes 1835024 | tf_op jit(solution)/shard_map/all_gather | solution.py:27
  717.4 39.0 %all-gather.41.cloned.1.call-done = bf16[1792,1216]{1,0:T(8,128)(2,1)} async-done(((bf16[224,1216]{1,0:T(8,128)(2,1)}), bf16[1792,1216]{1,0:T(8,128)(2,1)}) %all-gather.41.cloned.1.call-update) | async-done | bytes 4358160 | tf_op jit(solution)/shard_map/all_gather | solution.py:72
  756.4 8.9 multiply_convert_fusion.2
  776.1 23.8 all-gather.35.cloned.1.call-done
  799.9 6.9 fusion.137
  813.2 28.4 %all-gather.63.cloned.1.call-done = bf16[1,512,1792]{2,1,0:T(8,128)(2,1)} async-done(((bf16[1,128,1792]{2,1,0:T(8,128)(2,1)}), bf16[1,512,1792]{2,1,0:T(8,128)(2,1)}) %all-gather.63.cloned.1.call-update) | async-done | bytes 1835024 | tf_op jit(solution)/shard_map/all_gather | solution.py:27
  841.6 8.9 multiply_convert_fusion.6
  856.3 7.3 convolution_add_fusion.10
  863.7 48.1 %reduce-scatter.54.cloned.1.call-done = f32[128,1792]{1,0:T(8,128)} async-done(((f32[512,1792]{1,0:T(8,128)}), f32[128,1792]{1,0:T(8,128)}) %reduce-scatter.54.cloned.1.call-update) | async-done | bytes 917520 | tf_op jit(solution)/shard_map/reduce_scatter | solution.py:35
  911.8 71.0 %reduce-scatter.46.cloned.1.call-done = f32[128,1792]{1,0:T(8,128)} async-done(((f32[512,1792]{1,0:T(8,128)}), f32[128,1792]{1,0:T(8,128)}) %reduce-scatter.46.cloned.1.call-update) | async-done | bytes 917520 | tf_op jit(solution)/shard_map/reduce_scatter | solution.py:35
  989.2 39.8 %all-gather.45.cloned.1.call-done = bf16[512,1792]{1,0:T(8,128)(2,1)} async-done(((bf16[128,1792]{1,0:T(8,128)(2,1)}), bf16[512,1792]{1,0:T(8,128)(2,1)}) %all-gather.45.cloned.1.call-update) | async-done | bytes 1835024 | tf_op jit(solution)/shard_map/all_gather | solution.py:23
  1029.1 6.9 fusion.143
  1042.4 28.5 %all-gather.65.cloned.1.call-done = bf16[1,512,1792]{2,1,0:T(8,128)(2,1)} async-done(((bf16[1,128,1792]{2,1,0:T(8,128)(2,1)}), bf16[1,512,1792]{2,1,0:T(8,128)(2,1)}) %all-gather.65.cloned.1.call-update) | async-done | bytes 1835024 | tf_op jit(solution)/shard_map/all_gather | solution.py:27
  1070.9 8.9 multiply_convert_fusion.4
  1085.6 7.0 convolution_add_fusion.9
  1092.7 20.1 all-gather.53.cloned.1.call-done
  1112.8 6.9 fusion.154
  1126.2 28.4 %all-gather.69.cloned.1.call-done = bf16[1,512,1792]{2,1,0:T(8,128)(2,1)} async-done(((bf16[1,128,1792]{2,1,0:T(8,128)(2,1)}), bf16[1,512,1792]{2,1,0:T(8,128)(2,1)}) %all-gather.69.cloned.1.call-update) | async-done | bytes 1835024 | tf_op jit(solution)/shard_map/all_gather | solution.py:27
  1154.5 8.9 multiply_convert_fusion
  1169.3 7.1 convolution_add_fusion.7
  1176.4 7.2 fusion.145
  1183.7 7.2 fusion.156
  1191.0 33.7 %reduce-scatter.50.cloned.1.call-done = f32[128,1792]{1,0:T(8,128)} async-done(((f32[512,1792]{1,0:T(8,128)}), f32[128,1792]{1,0:T(8,128)}) %reduce-scatter.50.cloned.1.call-update) | async-done | bytes 917520 | tf_op jit(solution)/shard_map/reduce_scatter | solution.py:35
  1224.7 71.0 %reduce-scatter.58.cloned.1.call-done = f32[128,1792]{1,0:T(8,128)} async-done(((f32[512,1792]{1,0:T(8,128)}), f32[128,1792]{1,0:T(8,128)}) %reduce-scatter.58.cloned.1.call-update) | async-done | bytes 917520 | tf_op jit(solution)/shard_map/reduce_scatter | solution.py:35
  1300.2 66.5 %reduce-scatter.36.cloned.1.call-done = f32[128,1792]{1,0:T(8,128)} async-done(((f32[512,1792]{1,0:T(8,128)}), f32[128,1792]{1,0:T(8,128)}) %reduce-scatter.36.cloned.1.call-update) | async-done | bytes 917520 | tf_op jit(solution)/shard_map/reduce_scatter | solution.py:31
  1366.7 71.1 %reduce-scatter.44.cloned.1.call-done = f32[128,1792]{1,0:T(8,128)} async-done(((f32[512,1792]{1,0:T(8,128)}), f32[128,1792]{1,0:T(8,128)}) %reduce-scatter.44.cloned.1.call-update) | async-done | bytes 917520 | tf_op jit(solution)/shard_map/reduce_scatter | solution.py:31
  1447.2 38.1 %all-gather.61.cloned.1.call-done = bf16[512,1792]{1,0:T(8,128)(2,1)} async-done(((bf16[128,1792]{1,0:T(8,128)(2,1)}), bf16[512,1792]{1,0:T(8,128)(2,1)}) %all-gather.61.cloned.1.call-update) | async-done | bytes 1835024 | tf_op jit(solution)/shard_map/all_gather | solution.py:27
  1491.2 35.9 %all-gather.57.cloned.1.call-done = bf16[512,1792]{1,0:T(8,128)(2,1)} async-done(((bf16[128,1792]{1,0:T(8,128)(2,1)}), bf16[512,1792]{1,0:T(8,128)(2,1)}) %all-gather.57.cloned.1.call-update) | async-done | bytes 1835024 | tf_op jit(solution)/shard_map/all_gather | solution.py:27
  1532.5 36.5 %all-gather.59.cloned.1.call-done = bf16[512,1792]{1,0:T(8,128)(2,1)} async-done(((bf16[128,1792]{1,0:T(8,128)(2,1)}), bf16[512,1792]{1,0:T(8,128)(2,1)}) %all-gather.59.cloned.1.call-update) | async-done | bytes 1835024 | tf_op jit(solution)/shard_map/all_gather | solution.py:27
  1574.8 36.6 %all-gather.55.cloned.1.call-done = bf16[512,1792]{1,0:T(8,128)(2,1)} async-done(((bf16[128,1792]{1,0:T(8,128)(2,1)}), bf16[512,1792]{1,0:T(8,128)(2,1)}) %all-gather.55.cloned.1.call-update) | async-done | bytes 1835024 | tf_op jit(solution)/shard_map/all_gather | solution.py:27
  1666.5 49.7 %all-reduce.22.cloned.1.call-done = (bf16[32,2,448]{2,0,1:T(8,128)(2,1)}, bf16[32,2,448]{2,0,1:T(8,128)(2,1)}, bf16[32,2,448]{2,0,1:T(8,128)(2,1)}, bf16[32,2,448]{2,0,1:T(8,128)(2,1)}) async-done(((bf16[32,2,448]{2,0,1:T(8,128)(2,1)}, bf16[32,2,448]{2,0,1:T(8,128)(2,1)}, bf16[32,2,448]{2,0,1:T(8,128)(2,1)}, bf16[32,2,448]{2,0,1:T(8,128)(2,1)}), (bf16[32,2,448]{2,0,1:T(8,128)(2,1)}, ...) | async-done | bytes 229392
  1806.7 12.7 add_add_fusion.1
  1836.7 12.9 add_add_fusion
  1866.0 10.8 copy.122
  1909.6 24.7 reduce-scatter.52.cloned.1.call-done
  1934.3 71.1 %reduce-scatter.48.cloned.1.call-done = f32[128,1792]{1,0:T(8,128)} async-done(((f32[512,1792]{1,0:T(8,128)}), f32[128,1792]{1,0:T(8,128)}) %reduce-scatter.48.cloned.1.call-update) | async-done | bytes 917520 | tf_op jit(solution)/shard_map/reduce_scatter | solution.py:35
  2008.4 25.0 all-reduce.17
  2033.6 11.9 all-reduce.18
  2047.4 29.5 %reduce-scatter.40.cloned.1.call-done = f32[128,1792]{1,0:T(8,128)} async-done(((f32[512,1792]{1,0:T(8,128)}), f32[128,1792]{1,0:T(8,128)}) %reduce-scatter.40.cloned.1.call-update) | async-done | bytes 917520 | tf_op jit(solution)/shard_map/reduce_scatter | solution.py:31
  2080.5 67.4 %reduce-scatter.32.cloned.1.call-done = f32[128,1792]{1,0:T(8,128)} async-done(((f32[512,1792]{1,0:T(8,128)}), f32[128,1792]{1,0:T(8,128)}) %reduce-scatter.32.cloned.1.call-update) | async-done | bytes 917520 | tf_op jit(solution)/shard_map/reduce_scatter | solution.py:31
  2158.3 69.7 %reduce-scatter.68.cloned.1.call-done = f32[224,1216]{1,0:T(8,128)} async-done(((f32[1792,1216]{1,0:T(8,128)}), f32[224,1216]{1,0:T(8,128)}) %reduce-scatter.68.cloned.1.call-update) | async-done | bytes 1089552 | tf_op jit(solution)/shard_map/reduce_scatter | solution.py:196
  2228.0 79.3 %reduce-scatter.70.cloned.1.call-done = f32[224,1216]{1,0:T(8,128)} async-done(((f32[1792,1216]{1,0:T(8,128)}), f32[224,1216]{1,0:T(8,128)}) %reduce-scatter.70.cloned.1.call-update) | async-done | bytes 1089552 | tf_op jit(solution)/shard_map/reduce_scatter | solution.py:197
  2307.3 79.7 %reduce-scatter.72.cloned.1.call-done = f32[224,1216]{1,0:T(8,128)} async-done(((f32[1792,1216]{1,0:T(8,128)}), f32[224,1216]{1,0:T(8,128)}) %reduce-scatter.72.cloned.1.call-update) | async-done | bytes 1089552
  2387.0 52.6 %reduce-scatter.64.cloned.1.call-done = f32[224,448]{1,0:T(8,128)} async-done(((f32[1792,448]{1,0:T(8,128)}), f32[224,448]{1,0:T(8,128)}) %reduce-scatter.64.cloned.1.call-update) | async-done | bytes 401424 | tf_op jit(solution)/shard_map/reduce_scatter | solution.py:192
  2439.6 53.2 %reduce-scatter.66.cloned.1.call-done = f32[224,448]{1,0:T(8,128)} async-done(((f32[1792,448]{1,0:T(8,128)}), f32[224,448]{1,0:T(8,128)}) %reduce-scatter.66.cloned.1.call-update) | async-done | bytes 401424 | tf_op jit(solution)/shard_map/reduce_scatter | solution.py:194
  2492.8 52.6 %reduce-scatter.62.cloned.1.call-done = f32[224,448]{1,0:T(8,128)} async-done(((f32[1792,448]{1,0:T(8,128)}), f32[224,448]{1,0:T(8,128)}) %reduce-scatter.62.cloned.1.call-update) | async-done | bytes 401424 | tf_op jit(solution)/shard_map/reduce_scatter | solution.py:191
  (684 shorter events, 433.4 us)
Async XLA Ops:
  7.2 48.0 %all-gather.27.cloned.1.call-start = ((), (), s32[]{:S(2)}) async-start(), calls=%async_computation.22 | async-start | bytes 2293760 | tf_op jit(solution)/shard_map/all_gather | solution.py:23
  11.0 71.8 %all-gather.29.cloned.1.call-start = ((), (), s32[]{:S(2)}) async-start(), calls=%async_computation.23 | async-start | bytes 2064384 | tf_op jit(solution)/shard_map/all_gather | solution.py:67
  11.7 114.7 %all-gather.43.cloned.1.call-start = ((), (), s32[]{:S(2)}) async-start(), calls=%async_computation.32 | async-start | bytes 2293760 | tf_op jit(solution)/shard_map/all_gather | solution.py:23
  12.5 141.7 %all-gather.31.cloned.1.call-start = ((), (), s32[]{:S(2)}) async-start(), calls=%async_computation.24 | async-start | bytes 2064384 | tf_op jit(solution)/shard_map/all_gather | solution.py:68
  13.0 169.7 %all-gather.33.cloned.1.call-start = ((), (), s32[]{:S(2)}) async-start(), calls=%async_computation.25 | async-start | bytes 2064384 | tf_op jit(solution)/shard_map/all_gather | solution.py:71
  13.6 212.6 %all-gather.47.cloned.1.call-start = ((), (), s32[]{:S(2)}) async-start(), calls=%async_computation.36 | async-start | bytes 2293760 | tf_op jit(solution)/shard_map/all_gather | solution.py:23
  14.2 253.9 %all-gather.51.cloned.1.call-start = ((), (), s32[]{:S(2)}) async-start(), calls=%async_computation.40 | async-start | bytes 2293760 | tf_op jit(solution)/shard_map/all_gather | solution.py:23
  15.0 323.3 %reduce-scatter.30.cloned.1.call-start = ((), (), s32[]{:S(2)}) async-start(), calls=%async_computation.26 | async-start | bytes 4587520 | tf_op jit(solution)/shard_map/reduce_scatter | solution.py:31
  17.1 279.7 %copy-start.105 = (f32[1,448]{1,0:T(1,128)}, f32[1,448]{1,0:T(1,128)S(1)}, u32[]{:S(2)}) copy-start(f32[1,448]{1,0:T(1,128)S(1)} %get-tuple-element.208) | copy-start | bytes 5380
  17.1 279.7 %copy-start.107 = (f32[1,448]{1,0:T(1,128)}, f32[1,448]{1,0:T(1,128)S(1)}, u32[]{:S(2)}) copy-start(f32[1,448]{1,0:T(1,128)S(1)} %get-tuple-element.209) | copy-start | bytes 5380
  17.1 279.7 %copy-start.109 = (f32[1,448]{1,0:T(1,128)}, f32[1,448]{1,0:T(1,128)S(1)}, u32[]{:S(2)}) copy-start(f32[1,448]{1,0:T(1,128)S(1)} %get-tuple-element.210) | copy-start | bytes 5380
  17.9 139.6 %copy-start.97 = (f32[512]{0:T(512)}, f32[512]{0:T(512)S(1)}, u32[]{:S(2)}) copy-start(f32[512]{0:T(512)S(1)} %get-tuple-element.240) | copy-start | bytes 6148
  17.9 139.6 %copy-start.99 = (f32[512]{0:T(512)}, f32[512]{0:T(512)S(1)}, u32[]{:S(2)}) copy-start(f32[512]{0:T(512)S(1)} %get-tuple-element.241) | copy-start | bytes 6148
  18.0 139.5 %copy-start.101 = (f32[512]{0:T(512)}, f32[512]{0:T(512)S(1)}, u32[]{:S(2)}) copy-start(f32[512]{0:T(512)S(1)} %get-tuple-element.242) | copy-start | bytes 6148
  163.2 146.9 %copy-start.47 = (bf16[512,448]{0,1:T(8,128)(2,1)}, bf16[512,448]{0,1:T(8,128)(2,1)S(1)}, u32[]{:S(2)}) copy-start(bf16[512,448]{0,1:T(8,128)(2,1)S(1)} %get-tuple-element.220) | copy-start | bytes 1376260
  187.5 221.9 %reduce-scatter.38.cloned.1.call-start = ((), (), s32[]{:S(2)}) async-start(), calls=%async_computation.37 | async-start | bytes 4587520 | tf_op jit(solution)/shard_map/reduce_scatter | solution.py:31
  305.9 174.4 %reduce-scatter.42.cloned.1.call-start = ((), (), s32[]{:S(2)}) async-start(), calls=%async_computation.41 | async-start | bytes 4587520 | tf_op jit(solution)/shard_map/reduce_scatter | solution.py:31
  310.0 241.5 %reduce-scatter.34.cloned.1.call-start = ((), (), s32[]{:S(2)}) async-start(), calls=%async_computation.33 | async-start | bytes 4587520 | tf_op jit(solution)/shard_map/reduce_scatter | solution.py:31
  313.1 278.9 %all-gather.37.cloned.1.call-start = ((), (), s32[]{:S(2)}) async-start(), calls=%async_computation.28 | async-start | bytes 5160960 | tf_op jit(solution)/shard_map/all_gather | solution.py:69
  313.7 243.0 %copy-start.93 = (f32[1792]{0:T(1024)S(1)}, f32[1792]{0:T(1024)}, u32[]{:S(2)}) copy-start(f32[1792]{0:T(1024)} %param.26) | copy-start | bytes 21508
  313.7 321.9 %all-gather.49.cloned.1.call-start = ((), (), s32[]{:S(2)}) async-start(), calls=%async_computation.38 | async-start | bytes 2293760 | tf_op jit(solution)/shard_map/all_gather | solution.py:23
  555.8 739.9 %copy-start.10 = (f32[128,1792]{1,0:T(8,128)}, f32[128,1792]{1,0:T(8,128)S(1)}, u32[]{:S(2)}) copy-start(f32[128,1792]{1,0:T(8,128)S(1)} %get-tuple-element.117) | copy-start | bytes 2752516
  555.8 739.9 %copy-start.115 = (f32[128]{0:T(128)}, f32[128]{0:T(128)S(1)}, u32[]{:S(2)}) copy-start(f32[128]{0:T(128)S(1)} %add_rsqrt_fusion.6) | copy-start | bytes 1540
  555.8 882.0 %copy-start.117 = (f32[128]{0:T(128)}, f32[128]{0:T(128)S(1)}, u32[]{:S(2)}) copy-start(f32[128]{0:T(128)S(1)} %add_rsqrt_fusion.2) | copy-start | bytes 1540
  557.9 116.7 %all-gather.39.cloned.1.call-start = ((), (), s32[]{:S(2)}) async-start(), calls=%async_computation.29 | async-start | bytes 5160960 | tf_op jit(solution)/shard_map/all_gather | solution.py:70
  558.5 158.9 %all-gather.67.cloned.1.call-start = ((), (), s32[]{:S(2)}) async-start(), calls=%async_computation.58 | async-start | bytes 2293760 | tf_op jit(solution)/shard_map/all_gather | solution.py:27
  561.3 195.1 %all-gather.41.cloned.1.call-start = ((), (), s32[]{:S(2)}) async-start(), calls=%async_computation.30 | async-start | bytes 5160960 | tf_op jit(solution)/shard_map/all_gather | solution.py:72
  561.9 238.0 %all-gather.35.cloned.1.call-start = ((), (), s32[]{:S(2)}) async-start(), calls=%async_computation.27 | async-start | bytes 2293760 | tf_op jit(solution)/shard_map/all_gather | solution.py:23
  562.5 279.1 %all-gather.63.cloned.1.call-start = ((), (), s32[]{:S(2)}) async-start(), calls=%async_computation.56 | async-start | bytes 2293760 | tf_op jit(solution)/shard_map/all_gather | solution.py:27
  563.0 348.7 %reduce-scatter.54.cloned.1.call-start = ((), (), s32[]{:S(2)}) async-start(), calls=%async_computation.50 | async-start | bytes 4587520 | tf_op jit(solution)/shard_map/reduce_scatter | solution.py:35
  776.0 206.7 %reduce-scatter.46.cloned.1.call-start = ((), (), s32[]{:S(2)}) async-start(), calls=%async_computation.44 | async-start | bytes 4587520 | tf_op jit(solution)/shard_map/reduce_scatter | solution.py:35
  863.6 165.5 %all-gather.45.cloned.1.call-start = ((), (), s32[]{:S(2)}) async-start(), calls=%async_computation.34 | async-start | bytes 2293760 | tf_op jit(solution)/shard_map/all_gather | solution.py:23
  863.7 574.1 %copy-start.119 = (f32[128]{0:T(128)}, f32[128]{0:T(128)S(1)}, u32[]{:S(2)}) copy-start(f32[128]{0:T(128)S(1)} %add_rsqrt_fusion.4) | copy-start | bytes 1540
  863.7 574.1 %copy-start.121 = (f32[128]{0:T(128)}, f32[128]{0:T(128)S(1)}, u32[]{:S(2)}) copy-start(f32[128]{0:T(128)S(1)} %add_rsqrt_fusion) | copy-start | bytes 1540
  987.1 83.8 %all-gather.65.cloned.1.call-start = ((), (), s32[]{:S(2)}) async-start(), calls=%async_computation.57 | async-start | bytes 2293760 | tf_op jit(solution)/shard_map/all_gather | solution.py:27
  987.9 124.9 %all-gather.53.cloned.1.call-start = ((), (), s32[]{:S(2)}) async-start(), calls=%async_computation.42 | async-start | bytes 2293760 | tf_op jit(solution)/shard_map/all_gather | solution.py:23
  988.6 165.9 %all-gather.69.cloned.1.call-start = ((), (), s32[]{:S(2)}) async-start(), calls=%async_computation.59 | async-start | bytes 2293760 | tf_op jit(solution)/shard_map/all_gather | solution.py:27
  989.2 235.5 %reduce-scatter.50.cloned.1.call-start = ((), (), s32[]{:S(2)}) async-start(), calls=%async_computation.47 | async-start | bytes 4587520 | tf_op jit(solution)/shard_map/reduce_scatter | solution.py:35
  1092.7 203.0 %reduce-scatter.58.cloned.1.call-start = ((), (), s32[]{:S(2)}) async-start(), calls=%async_computation.53 | async-start | bytes 4587520 | tf_op jit(solution)/shard_map/reduce_scatter | solution.py:35
  1176.4 190.3 %reduce-scatter.36.cloned.1.call-start = ((), (), s32[]{:S(2)}) async-start(), calls=%async_computation.35 | async-start | bytes 4587520 | tf_op jit(solution)/shard_map/reduce_scatter | solution.py:31
  1183.6 254.2 %reduce-scatter.44.cloned.1.call-start = ((), (), s32[]{:S(2)}) async-start(), calls=%async_computation.43 | async-start | bytes 4587520 | tf_op jit(solution)/shard_map/reduce_scatter | solution.py:31
  1190.9 294.5 %all-gather.61.cloned.1.call-start = ((), (), s32[]{:S(2)}) async-start(), calls=%async_computation.54 | async-start | bytes 2293760 | tf_op jit(solution)/shard_map/all_gather | solution.py:27
  1191.0 246.8 %copy-start.151 = (f32[128]{0:T(128)}, f32[128]{0:T(128)S(1)}, u32[]{:S(2)}) copy-start(f32[128]{0:T(128)S(1)} %broadcast_multiply_fusion.7) | copy-start | bytes 1540
  1300.2 143.2 %copy-start.149 = (f32[128]{0:T(128)}, f32[128]{0:T(128)S(1)}, u32[]{:S(2)}) copy-start(f32[128]{0:T(128)S(1)} %broadcast_multiply_fusion.5) | copy-start | bytes 1540
  1300.2 143.2 %copy-start.145 = (f32[128]{0:T(128)}, f32[128]{0:T(128)S(1)}, u32[]{:S(2)}) copy-start(f32[128]{0:T(128)S(1)} %broadcast_multiply_fusion.9) | copy-start | bytes 1540
  1443.4 83.6 %all-gather.57.cloned.1.call-start = ((), (), s32[]{:S(2)}) async-start(), calls=%async_computation.48 | async-start | bytes 2293760 | tf_op jit(solution)/shard_map/all_gather | solution.py:27
  1444.0 124.9 %all-gather.59.cloned.1.call-start = ((), (), s32[]{:S(2)}) async-start(), calls=%async_computation.51 | async-start | bytes 2293760 | tf_op jit(solution)/shard_map/all_gather | solution.py:27
  1444.7 166.6 %all-gather.55.cloned.1.call-start = ((), (), s32[]{:S(2)}) async-start(), calls=%async_computation.45 | async-start | bytes 2293760 | tf_op jit(solution)/shard_map/all_gather | solution.py:27
  1445.5 270.7 %all-reduce.22.cloned.1.call-start = ((), (), s32[]{:S(2)}) async-start(), calls=%async_computation.66 | async-start | bytes 524288
  1663.1 246.5 %reduce-scatter.56.cloned.1.call-start = ((), (), s32[]{:S(2)}) async-start(), calls=%async_computation.52 | async-start | bytes 4587520 | tf_op jit(solution)/shard_map/reduce_scatter | solution.py:35
  1724.1 185.5 %reduce-scatter.60.cloned.1.call-start = ((), (), s32[]{:S(2)}) async-start(), calls=%async_computation.55 | async-start | bytes 4587520 | tf_op jit(solution)/shard_map/reduce_scatter | solution.py:35
  1741.4 192.9 %reduce-scatter.52.cloned.1.call-start = ((), (), s32[]{:S(2)}) async-start(), calls=%async_computation.49 | async-start | bytes 4587520 | tf_op jit(solution)/shard_map/reduce_scatter | solution.py:35
  1757.9 247.4 %reduce-scatter.48.cloned.1.call-start = ((), (), s32[]{:S(2)}) async-start(), calls=%async_computation.46 | async-start | bytes 4587520 | tf_op jit(solution)/shard_map/reduce_scatter | solution.py:35
  1772.8 304.0 %reduce-scatter.40.cloned.1.call-start = ((), (), s32[]{:S(2)}) async-start(), calls=%async_computation.39 | async-start | bytes 4587520 | tf_op jit(solution)/shard_map/reduce_scatter | solution.py:31
  1780.8 367.1 %reduce-scatter.32.cloned.1.call-start = ((), (), s32[]{:S(2)}) async-start(), calls=%async_computation.31 | async-start | bytes 4587520 | tf_op jit(solution)/shard_map/reduce_scatter | solution.py:31
  1788.8 439.2 %reduce-scatter.68.cloned.1.call-start = ((), (), s32[]{:S(2)}) async-start(), calls=%async_computation.63 | async-start | bytes 10321920 | tf_op jit(solution)/shard_map/reduce_scatter | solution.py:196
  1819.4 487.9 %reduce-scatter.70.cloned.1.call-start = ((), (), s32[]{:S(2)}) async-start(), calls=%async_computation.64 | async-start | bytes 10321920 | tf_op jit(solution)/shard_map/reduce_scatter | solution.py:197
  1849.6 537.4 %reduce-scatter.72.cloned.1.call-start = ((), (), s32[]{:S(2)}) async-start(), calls=%async_computation.65 | async-start | bytes 10321920
  1876.8 562.8 %reduce-scatter.64.cloned.1.call-start = ((), (), s32[]{:S(2)}) async-start(), calls=%async_computation.61 | async-start | bytes 4128768 | tf_op jit(solution)/shard_map/reduce_scatter | solution.py:192
  1886.8 606.0 %reduce-scatter.66.cloned.1.call-start = ((), (), s32[]{:S(2)}) async-start(), calls=%async_computation.62 | async-start | bytes 4128768 | tf_op jit(solution)/shard_map/reduce_scatter | solution.py:194
  1896.9 648.5 %reduce-scatter.62.cloned.1.call-start = ((), (), s32[]{:S(2)}) async-start(), calls=%async_computation.60 | async-start | bytes 4128768 | tf_op jit(solution)/shard_map/reduce_scatter | solution.py:191
  1909.5 167.3 %copy-start.94 = (f32[1792]{0:T(1024)S(1)}, f32[1792]{0:T(1024)}, u32[]{:S(2)}) copy-start(f32[1792]{0:T(1024)} %param.26) | copy-start | bytes 21508
  1909.5 167.3 %copy-start.118 = (f32[128]{0:T(128)S(1)}, f32[128]{0:T(128)}, u32[]{:S(2)}) copy-start(f32[128]{0:T(128)} %copy-done.117) | copy-start | bytes 1540
  1909.5 167.3 %copy-start.152 = (f32[128]{0:T(128)S(1)}, f32[128]{0:T(128)}, u32[]{:S(2)}) copy-start(f32[128]{0:T(128)} %copy-done.151) | copy-start | bytes 1540
  (165 other events, 2166.2 us)
Sparse Core Ops, SparseCore 0:
  11.1 44.0 all-gather.26
  57.1 25.6 all-gather.28
  85.0 41.3 all-gather.42
  128.1 26.0 all-gather.30
  155.9 26.7 all-gather.32
  184.8 41.4 all-gather.46
  227.8 40.2 all-gather.50
  270.9 67.2 reduce-scatter.29
  340.6 68.7 reduce-scatter.37
  411.5 68.7 reduce-scatter.41
  482.7 68.7 reduce-scatter.33
  553.2 38.7 all-gather.36
  594.1 41.3 all-gather.48
  637.3 37.2 all-gather.38
  676.0 41.3 all-gather.66
  719.2 37.2 all-gather.40
  758.4 41.3 all-gather.34
  801.3 40.2 all-gather.62
  844.5 67.2 reduce-scatter.53
  913.9 68.7 reduce-scatter.45
  987.3 41.7 all-gather.44
  1030.6 40.2 all-gather.64
  1072.5 40.2 all-gather.52
  1114.2 40.2 all-gather.68
  1157.4 67.2 reduce-scatter.49
  1226.9 68.7 reduce-scatter.57
  1297.8 68.7 reduce-scatter.35
  1369.0 68.7 reduce-scatter.43
  1443.5 41.7 all-gather.60
  1486.8 40.2 all-gather.56
  1528.6 40.2 all-gather.58
  1571.1 40.2 all-gather.54
  1663.2 52.9 all-reduce.21
  1724.2 67.7 reduce-scatter.55
  1794.4 68.7 reduce-scatter.59
  1865.5 68.7 reduce-scatter.51
  1936.5 68.7 reduce-scatter.47
  2007.8 69.0 reduce-scatter.39
  2079.1 68.7 reduce-scatter.31
  2152.6 75.4 reduce-scatter.67
  2232.2 75.0 reduce-scatter.69
  2311.9 75.0 reduce-scatter.71
  2390.9 48.6 reduce-scatter.63
  2444.0 48.7 reduce-scatter.65
  2496.7 48.7 reduce-scatter.61
where the time goes:
time: 2560 us; the launch traced here: 2550 us
  waiting for transfers between devices  1900 us (74%)
  matrix products  355 us (14%)
  local copies, waits for them, and re-layouts  126 us (5%)
  blocking collectives  74 us (3%)
  other arithmetic  71.4 us (3%)
    reduce_scatter x8, waiting for transfers between devices, collect(): return lax.psum_scatter(partial_sum, 'col', scatter_dimension=0, tiled=True)  472 us
    reduce_scatter x8, waiting for transfers between devices, collect_grad(): return lax.psum_scatter(partial_sum, 'col', scatter_dimension=0, tiled=True)  320 us
    all_gather x8, waiting for transfers between devices, spread_grad(): return lax.all_gather(shard, 'col', axis=0, tiled=True)  268 us
    all_gather x8, waiting for transfers between devices, spread(): return lax.all_gather(shard, 'col', axis=0, tiled=True)  246 us
    unnamed x47, waiting for transfers between devices  140 us
    dot_general x24, matrix products, contract_last(): lax.dot_general(left, right, (((1,), (1,)), ((), ())), preferred_element_...  114 us
    dot_general x24, matrix products, contract_first(): lax.dot_general(left, right, (((0,), (0,)), ((), ())), preferred_element_...  98.6 us
    reduce_scatter x1, waiting for transfers between devices, per_device(): lax.psum_scatter(partials[7], 'row', scatter_dimension=0, tiled=True)  79.3 us
  transfers between devices with their start and end apart: 45, of which 43 were waited for; matrix products, arithmetic and copies ran while one was open for 18% of the time, Pallas kernels for 0%

commit v1 on v0

--- a/solution.py
+++ b/solution.py
@@ -1,3 +1,4 @@
+import functools
 import jax
 import jax.numpy as jnp
 from jax import lax
@@ -7,6 +8,27 @@
 EPSILON = 1e-05
 
 
+def lead_the_sample(t0, which_axis):
+    sides = lax.axis_size(which_axis)
+    buffer = [(t, (t + 1) % sides) for t in range(sides)]
+    vals = [(t, (t - 1) % sides) for t in range(sides)]
+    y2, known = ([t0], [t0])
+    for _ in range(sides // 2):
+        y2.append(lax.ppermute(y2[-1], perm=buffer, axis_name=which_axis))
+    jj = 0
+    while jj < (sides - 1) // 2:
+        known.append(lax.ppermute(known[-1], axis_name=which_axis, perm=vals))
+        jj += 1
+    return jnp.roll(
+        jnp.concatenate([*y2[::-1], *known[1:]], axis=0),
+        (lax.axis_index(which_axis) - sides // 2) * t0.shape[0],
+        axis=0,
+    )
+
+
+_assign_islands = functools.partial(lead_the_sample, which_axis="col")
+
+
 def contract_last(left, right):
     return lax.dot_general(
         left, right, (((1,), (1,)), ((), ())), preferred_element_type=jnp.float32
@@ -24,7 +46,7 @@
 
 
 def spread_grad(shard):
-    return lax.all_gather(shard, "col", axis=0, tiled=True)
+    return _assign_islands(shard)
 
 
 def collect(partial_sum):

time: 2560 us -> 2430 us (0.949)
  waiting for transfers between devices: 1900 us -> 1650 us
  starting transfers between devices: 4.43 us -> 97.8 us
  other arithmetic: 71.4 us -> 131 us
    all_gather x8 -> x0, waiting for transfers between devices: 268 us -> none  [spread_grad(): return lax.all_gather(shard, 'col', axis=0, tiled=True)]
    ppermute x0 -> x24, waiting for transfers between devices: none -> 202 us  [the longest x16 170 us: lead_the_sample(): y2.append(lax.ppermute(y2[-1], perm=buffer, axis_name=which_axis))]
    ppermute x0 -> x24, starting transfers between devices: none -> 94.7 us  [the longest x16 81.9 us: lead_the_sample(): y2.append(lax.ppermute(y2[-1], perm=buffer, axis_name=which_axis))]
    all_gather x8, waiting for transfers between devices: 246 us -> 153 us  [spread(): return lax.all_gather(shard, 'col', axis=0, tiled=True)]
    unnamed x47 -> x38, waiting for transfers between devices: 140 us -> 55.8 us
    reduce_scatter x0 -> x1, waiting for transfers between devices: none -> 79.7 us  [per_device(): lax.psum_scatter(partials[8], 'row', scatter_dimension=0, tiled=True)]
    concatenate x0 -> x8, other arithmetic: none -> 59.6 us  [lead_the_sample(): jnp.roll(jnp.concatenate([*y2[::-1], *known[1:]], axis=0), (lax.axis_inde...]
    reduce_scatter x8, waiting for transfers between devices: 320 us -> 264 us  [collect_grad(): return lax.psum_scatter(partial_sum, 'col', scatter_dimension=0, tiled=True)]
  transfers between devices with their start and end apart: 45 -> 61, of which waited for: 43 -> 51; matrix products, arithmetic and copies ran while one was open for 18% -> 20% of each run, Pallas kernels for 0% -> 0%
where the time goes in v1:
time: 2430 us; the launch traced here: 2420 us
  waiting for transfers between devices  1650 us (68%)
  matrix products  330 us (14%)
  other arithmetic  131 us (5%)
  local copies, waits for them, and re-layouts  116 us (5%)
  starting transfers between devices  97.8 us (4%)
  blocking collectives  74.1 us (3%)
    reduce_scatter x8, waiting for transfers between devices, collect(): return lax.psum_scatter(partial_sum, 'col', scatter_dimension=0, tiled=True)  473 us
    reduce_scatter x8, waiting for transfers between devices, collect_grad(): return lax.psum_scatter(partial_sum, 'col', scatter_dimension=0, tiled=True)  264 us
    ppermute x16, waiting for transfers between devices, lead_the_sample(): y2.append(lax.ppermute(y2[-1], perm=buffer, axis_name=which_axis))  170 us
    all_gather x8, waiting for transfers between devices, spread(): return lax.all_gather(shard, 'col', axis=0, tiled=True)  153 us
    dot_general x24, matrix products, contract_first(): lax.dot_general(left, right, (((0,), (0,)), ((), ())), preferred_element_...  114 us
    dot_general x24, matrix products, contract_last(): lax.dot_general(left, right, (((1,), (1,)), ((), ())), preferred_element_...  98.1 us
    ppermute x16, starting transfers between devices, lead_the_sample(): y2.append(lax.ppermute(y2[-1], perm=buffer, axis_name=which_axis))  81.9 us
    reduce_scatter x1, waiting for transfers between devices, per_device(): lax.psum_scatter(partials[8], 'row', scatter_dimension=0, tiled=True)  79.7 us
  transfers between devices with their start and end apart: 61, of which 51 were waited for; matrix products, arithmetic and copies ran while one was open for 20% of the time, Pallas kernels for 0%

profile of v1, /device:TPU:0, one launch (start us, length us, event | category | flops | bytes accessed | tf_op | source)
XLA Modules:
  0.0 2418.2 jit_solution(14620455577075247297)
XLA Ops:
  18.7 37.2 %all-gather.15.cloned.1.call-done = bf16[512,1792]{1,0:T(8,128)(2,1)} async-done(((bf16[128,1792]{1,0:T(8,128)(2,1)}), bf16[512,1792]{1,0:T(8,128)(2,1)}) %all-gather.15.cloned.1.call-update) | async-done | bytes 1835024 | tf_op jit(solution)/shard_map/all_gather | solution.py:45
  55.9 27.6 %all-gather.17.cloned.1.call-done = bf16[1792,448]{1,0:T(8,128)(2,1)} async-done(((bf16[224,448]{1,0:T(8,128)(2,1)}), bf16[1792,448]{1,0:T(8,128)(2,1)}) %all-gather.17.cloned.1.call-update) | async-done | bytes 1605648 | tf_op jit(solution)/shard_map/all_gather | solution.py:89
  92.0 9.2 all_gather.74
  103.0 24.0 all-gather.31.cloned.1.call-done
  135.1 9.6 all_gather.82
  163.8 19.6 all-gather.21.cloned.1.call-done
  190.8 36.1 %all-gather.35.cloned.1.call-done = bf16[512,1792]{1,0:T(8,128)(2,1)} async-done(((bf16[128,1792]{1,0:T(8,128)(2,1)}), bf16[512,1792]{1,0:T(8,128)(2,1)}) %all-gather.35.cloned.1.call-update) | async-done | bytes 1835024 | tf_op jit(solution)/shard_map/all_gather | solution.py:45
  235.4 9.3 all_gather.85
  246.7 22.0 all-gather.39.cloned.1.call-done
  279.4 9.1 all_gather.88
  314.2 24.6 %reduce-scatter.28.cloned.1.call-done = f32[128,1792]{1,0:T(8,128)} async-done(((f32[512,1792]{1,0:T(8,128)}), f32[128,1792]{1,0:T(8,128)}) %reduce-scatter.28.cloned.1.call-update) | async-done | bytes 917520 | tf_op jit(solution)/shard_map/reduce_scatter | solution.py:53
  338.9 71.1 %reduce-scatter.36.cloned.1.call-done = f32[128,1792]{1,0:T(8,128)} async-done(((f32[512,1792]{1,0:T(8,128)}), f32[128,1792]{1,0:T(8,128)}) %reduce-scatter.36.cloned.1.call-update) | async-done | bytes 917520 | tf_op jit(solution)/shard_map/reduce_scatter | solution.py:53
  410.0 71.0 %reduce-scatter.40.cloned.1.call-done = f32[128,1792]{1,0:T(8,128)} async-done(((f32[512,1792]{1,0:T(8,128)}), f32[128,1792]{1,0:T(8,128)}) %reduce-scatter.40.cloned.1.call-update) | async-done | bytes 917520 | tf_op jit(solution)/shard_map/reduce_scatter | solution.py:53
  481.0 71.1 %reduce-scatter.32.cloned.1.call-done = f32[128,1792]{1,0:T(8,128)} async-done(((f32[512,1792]{1,0:T(8,128)}), f32[128,1792]{1,0:T(8,128)}) %reduce-scatter.32.cloned.1.call-update) | async-done | bytes 917520 | tf_op jit(solution)/shard_map/reduce_scatter | solution.py:53
  566.2 11.8 collective-permute-done.12
  587.5 8.8 collective-permute-done.13
  602.9 33.4 %all-gather.37.cloned.1.call-done = bf16[512,1792]{1,0:T(8,128)(2,1)} async-done(((bf16[128,1792]{1,0:T(8,128)(2,1)}), bf16[512,1792]{1,0:T(8,128)(2,1)}) %all-gather.37.cloned.1.call-update) | async-done | bytes 1835024 | tf_op jit(solution)/shard_map/all_gather | solution.py:45
  643.0 32.2 %all-gather.27.cloned.1.call-done = bf16[1792,1216]{1,0:T(8,128)(2,1)} async-done(((bf16[224,1216]{1,0:T(8,128)(2,1)}), bf16[1792,1216]{1,0:T(8,128)(2,1)}) %all-gather.27.cloned.1.call-update) | async-done | bytes 4358160 | tf_op jit(solution)/shard_map/all_gather | solution.py:92
  682.0 33.3 %all-gather.29.cloned.1.call-done = bf16[1792,1216]{1,0:T(8,128)(2,1)} async-done(((bf16[224,1216]{1,0:T(8,128)(2,1)}), bf16[1792,1216]{1,0:T(8,128)(2,1)}) %all-gather.29.cloned.1.call-update) | async-done | bytes 4358160 | tf_op jit(solution)/shard_map/all_gather | solution.py:94
  715.4 8.9 multiply_convert_fusion.2
  738.9 21.4 collective-permute-done
  760.3 14.2 collective-permute-start.1
  776.5 12.3 collective-permute-done.1
  788.8 7.9 fusion.52
  822.6 26.4 %reduce-scatter.52.cloned.1.call-done = f32[128,1792]{1,0:T(8,128)} async-done(((f32[512,1792]{1,0:T(8,128)}), f32[128,1792]{1,0:T(8,128)}) %reduce-scatter.52.cloned.1.call-update) | async-done | bytes 917520 | tf_op jit(solution)/shard_map/reduce_scatter | solution.py:57
  849.0 70.4 %reduce-scatter.44.cloned.1.call-done = f32[128,1792]{1,0:T(8,128)} async-done(((f32[512,1792]{1,0:T(8,128)}), f32[128,1792]{1,0:T(8,128)}) %reduce-scatter.44.cloned.1.call-update) | async-done | bytes 917520 | tf_op jit(solution)/shard_map/reduce_scatter | solution.py:57
  927.8 14.4 collective-permute-done.6
  942.1 11.2 collective-permute-start.7
  953.3 21.4 collective-permute-done.8
  980.1 7.9 fusion.38
  1020.5 20.7 collective-permute-done.18
  1041.2 9.0 collective-permute-start.19
  1053.2 13.9 collective-permute-done.19
  1067.1 8.6 fusion.10
  1116.4 8.3 reduce-scatter.48.cloned.1.call-done
  1124.7 69.4 %reduce-scatter.56.cloned.1.call-done = f32[128,1792]{1,0:T(8,128)} async-done(((f32[512,1792]{1,0:T(8,128)}), f32[128,1792]{1,0:T(8,128)}) %reduce-scatter.56.cloned.1.call-update) | async-done | bytes 917520 | tf_op jit(solution)/shard_map/reduce_scatter | solution.py:57
  1197.9 67.4 %reduce-scatter.34.cloned.1.call-done = f32[128,1792]{1,0:T(8,128)} async-done(((f32[512,1792]{1,0:T(8,128)}), f32[128,1792]{1,0:T(8,128)}) %reduce-scatter.34.cloned.1.call-update) | async-done | bytes 917520 | tf_op jit(solution)/shard_map/reduce_scatter | solution.py:53
  1265.2 71.0 %reduce-scatter.42.cloned.1.call-done = f32[128,1792]{1,0:T(8,128)} async-done(((f32[512,1792]{1,0:T(8,128)}), f32[128,1792]{1,0:T(8,128)}) %reduce-scatter.42.cloned.1.call-update) | async-done | bytes 917520 | tf_op jit(solution)/shard_map/reduce_scatter | solution.py:53
  1345.5 11.8 collective-permute-done.21
  1357.2 8.7 collective-permute-start.22
  1377.0 9.7 collective-permute-done.22
  1386.8 8.6 collective-permute-start.16
  1406.4 8.6 collective-permute-start.4
  1415.0 11.2 collective-permute-done.9
  1426.2 9.7 collective-permute-done.16
  1435.9 8.0 fusion.17
  1444.0 11.5 collective-permute-done.4
  1466.1 8.0 fusion.31
  1531.7 50.1 %all-reduce.22.cloned.1.call-done = (bf16[32,2,448]{2,0,1:T(8,128)(2,1)}, bf16[32,2,448]{2,0,1:T(8,128)(2,1)}, bf16[32,2,448]{2,0,1:T(8,128)(2,1)}, bf16[32,2,448]{2,0,1:T(8,128)(2,1)}) async-done(((bf16[32,2,448]{2,0,1:T(8,128)(2,1)}, bf16[32,2,448]{2,0,1:T(8,128)(2,1)}, bf16[32,2,448]{2,0,1:T(8,128)(2,1)}, bf16[32,2,448]{2,0,1:T(8,128)(2,1)}), (bf16[32,2,448]{2,0,1:T(8,128)(2,1)}, ...) | async-done | bytes 229392
  1673.6 12.8 add_add_fusion.2
  1703.8 12.7 add_add_fusion.1
  1734.4 13.8 add_add_fusion
  1781.3 18.5 reduce-scatter.50.cloned.1.call-done
  1799.8 71.2 %reduce-scatter.46.cloned.1.call-done = f32[128,1792]{1,0:T(8,128)} async-done(((f32[512,1792]{1,0:T(8,128)}), f32[128,1792]{1,0:T(8,128)}) %reduce-scatter.46.cloned.1.call-update) | async-done | bytes 917520 | tf_op jit(solution)/shard_map/reduce_scatter | solution.py:57
  1874.1 25.0 %all-reduce.17 = (f32[1792]{0:T(1024)S(1)}, f32[3,448]{1,0:T(4,128)S(1)}, f32[1792]{0:T(1024)S(1)}) all-reduce(f32[1792]{0:T(1024)S(1)} %add_add_fusion.7, f32[3,448]{1,0:T(4,128)S(1)} %fusion.152, f32[1792]{0:T(1024)S(1)} %add_add_fusion.6), channel_id=49, replica_groups=mesh['row'=8,'col'=4] {'row'}, use_global_device_ids=true, to_apply=%region_53.57.clone | all-reduce | flops 4928 | bytes 39424
  1899.3 11.8 all-reduce.18
  1913.0 29.4 %reduce-scatter.38.cloned.1.call-done = f32[128,1792]{1,0:T(8,128)} async-done(((f32[512,1792]{1,0:T(8,128)}), f32[128,1792]{1,0:T(8,128)}) %reduce-scatter.38.cloned.1.call-update) | async-done | bytes 917520 | tf_op jit(solution)/shard_map/reduce_scatter | solution.py:53
  1946.0 67.6 %reduce-scatter.30.cloned.1.call-done = f32[128,1792]{1,0:T(8,128)} async-done(((f32[512,1792]{1,0:T(8,128)}), f32[128,1792]{1,0:T(8,128)}) %reduce-scatter.30.cloned.1.call-update) | async-done | bytes 917520 | tf_op jit(solution)/shard_map/reduce_scatter | solution.py:53
  2023.9 69.8 %reduce-scatter.66.cloned.1.call-done = f32[224,1216]{1,0:T(8,128)} async-done(((f32[1792,1216]{1,0:T(8,128)}), f32[224,1216]{1,0:T(8,128)}) %reduce-scatter.66.cloned.1.call-update) | async-done | bytes 1089552 | tf_op jit(solution)/shard_map/reduce_scatter | solution.py:218
  2093.7 79.1 %reduce-scatter.68.cloned.1.call-done = f32[224,1216]{1,0:T(8,128)} async-done(((f32[1792,1216]{1,0:T(8,128)}), f32[224,1216]{1,0:T(8,128)}) %reduce-scatter.68.cloned.1.call-update) | async-done | bytes 1089552 | tf_op jit(solution)/shard_map/reduce_scatter | solution.py:219
  2172.8 79.7 %reduce-scatter.70.cloned.1.call-done = f32[224,1216]{1,0:T(8,128)} async-done(((f32[1792,1216]{1,0:T(8,128)}), f32[224,1216]{1,0:T(8,128)}) %reduce-scatter.70.cloned.1.call-update) | async-done | bytes 1089552 | tf_op jit(solution)/shard_map/reduce_scatter | solution.py:220
  2252.5 52.8 %reduce-scatter.62.cloned.1.call-done = f32[224,448]{1,0:T(8,128)} async-done(((f32[1792,448]{1,0:T(8,128)}), f32[224,448]{1,0:T(8,128)}) %reduce-scatter.62.cloned.1.call-update) | async-done | bytes 401424 | tf_op jit(solution)/shard_map/reduce_scatter | solution.py:214
  2305.3 53.0 %reduce-scatter.64.cloned.1.call-done = f32[224,448]{1,0:T(8,128)} async-done(((f32[1792,448]{1,0:T(8,128)}), f32[224,448]{1,0:T(8,128)}) %reduce-scatter.64.cloned.1.call-update) | async-done | bytes 401424 | tf_op jit(solution)/shard_map/reduce_scatter | solution.py:216
  2358.3 52.6 %reduce-scatter.60.cloned.1.call-done = f32[224,448]{1,0:T(8,128)} async-done(((f32[1792,448]{1,0:T(8,128)}), f32[224,448]{1,0:T(8,128)}) %reduce-scatter.60.cloned.1.call-update) | async-done | bytes 401424 | tf_op jit(solution)/shard_map/reduce_scatter | solution.py:213
  (800 shorter events, 556.2 us)
Async XLA Ops:
  7.2 48.7 %all-gather.15.cloned.1.call-start = ((), (), s32[]{:S(2)}) async-start(), calls=%async_computation.22 | async-start | bytes 2293760 | tf_op jit(solution)/shard_map/all_gather | solution.py:45
  11.6 71.8 %all-gather.17.cloned.1.call-start = ((), (), s32[]{:S(2)}) async-start(), calls=%async_computation.23 | async-start | bytes 2064384 | tf_op jit(solution)/shard_map/all_gather | solution.py:89
  12.4 114.7 %all-gather.31.cloned.1.call-start = ((), (), s32[]{:S(2)}) async-start(), calls=%async_computation.32 | async-start | bytes 2293760 | tf_op jit(solution)/shard_map/all_gather | solution.py:45
  13.1 141.7 %all-gather.19.cloned.1.call-start = ((), (), s32[]{:S(2)}) async-start(), calls=%async_computation.24 | async-start | bytes 2064384 | tf_op jit(solution)/shard_map/all_gather | solution.py:90
  13.7 169.7 %all-gather.21.cloned.1.call-start = ((), (), s32[]{:S(2)}) async-start(), calls=%async_computation.25 | async-start | bytes 2064384 | tf_op jit(solution)/shard_map/all_gather | solution.py:93
  14.3 212.6 %all-gather.35.cloned.1.call-start = ((), (), s32[]{:S(2)}) async-start(), calls=%async_computation.36 | async-start | bytes 2293760 | tf_op jit(solution)/shard_map/all_gather | solution.py:45
  14.9 253.9 %all-gather.39.cloned.1.call-start = ((), (), s32[]{:S(2)}) async-start(), calls=%async_computation.40 | async-start | bytes 2293760 | tf_op jit(solution)/shard_map/all_gather | solution.py:45
  15.6 323.3 %reduce-scatter.28.cloned.1.call-start = ((), (), s32[]{:S(2)}) async-start(), calls=%async_computation.26 | async-start | bytes 4587520 | tf_op jit(solution)/shard_map/reduce_scatter | solution.py:53
  188.1 221.9 %reduce-scatter.36.cloned.1.call-start = ((), (), s32[]{:S(2)}) async-start(), calls=%async_computation.37 | async-start | bytes 4587520 | tf_op jit(solution)/shard_map/reduce_scatter | solution.py:53
  306.5 174.5 %reduce-scatter.40.cloned.1.call-start = ((), (), s32[]{:S(2)}) async-start(), calls=%async_computation.41 | async-start | bytes 4587520 | tf_op jit(solution)/shard_map/reduce_scatter | solution.py:53
  310.5 241.6 %reduce-scatter.32.cloned.1.call-start = ((), (), s32[]{:S(2)}) async-start(), calls=%async_computation.33 | async-start | bytes 4587520 | tf_op jit(solution)/shard_map/reduce_scatter | solution.py:53
  313.6 289.2 %all-gather.25.cloned.1.call-start = ((), (), s32[]{:S(2)}) async-start(), calls=%async_computation.28 | async-start | bytes 5160960 | tf_op jit(solution)/shard_map/all_gather | solution.py:91
  314.2 322.0 %all-gather.37.cloned.1.call-start = ((), (), s32[]{:S(2)}) async-start(), calls=%async_computation.38 | async-start | bytes 2293760 | tf_op jit(solution)/shard_map/all_gather | solution.py:45
  556.4 637.7 %copy-start.10 = (f32[128,1792]{1,0:T(8,128)}, f32[128,1792]{1,0:T(8,128)S(1)}, u32[]{:S(2)}) copy-start(f32[128,1792]{1,0:T(8,128)S(1)} %get-tuple-element.74) | copy-start | bytes 2752516
  556.4 637.7 %copy-start.133 = (f32[128]{0:T(128)}, f32[128]{0:T(128)S(1)}, u32[]{:S(2)}) copy-start(f32[128]{0:T(128)S(1)} %add_rsqrt_fusion.6) | copy-start | bytes 1540
  556.4 779.8 %copy-start.135 = (f32[128]{0:T(128)}, f32[128]{0:T(128)S(1)}, u32[]{:S(2)}) copy-start(f32[128]{0:T(128)S(1)} %add_rsqrt_fusion.2) | copy-start | bytes 1540
  558.5 116.7 %all-gather.27.cloned.1.call-start = ((), (), s32[]{:S(2)}) async-start(), calls=%async_computation.29 | async-start | bytes 5160960 | tf_op jit(solution)/shard_map/all_gather | solution.py:92
  559.1 156.3 %all-gather.29.cloned.1.call-start = ((), (), s32[]{:S(2)}) async-start(), calls=%async_computation.30 | async-start | bytes 5160960 | tf_op jit(solution)/shard_map/all_gather | solution.py:94
  559.7 237.1 %all-gather.23.cloned.1.call-start = ((), (), s32[]{:S(2)}) async-start(), calls=%async_computation.27 | async-start | bytes 2293760 | tf_op jit(solution)/shard_map/all_gather | solution.py:45
  562.4 15.7 collective-permute-start.12
  563.6 23.8 collective-permute-start.14
  578.1 18.2 collective-permute-start.13
  602.4 246.6 %reduce-scatter.52.cloned.1.call-start = ((), (), s32[]{:S(2)}) async-start(), calls=%async_computation.48 | async-start | bytes 4587520 | tf_op jit(solution)/shard_map/reduce_scatter | solution.py:57
  734.9 184.5 %reduce-scatter.44.cloned.1.call-start = ((), (), s32[]{:S(2)}) async-start(), calls=%async_computation.44 | async-start | bytes 4587520 | tf_op jit(solution)/shard_map/reduce_scatter | solution.py:57
  735.0 25.3 %collective-permute-start = (bf16[128,1792]{1,0:T(8,128)(2,1)}, bf16[128,1792]{1,0:T(8,128)(2,1)S(1)}, u32[]{:S(2)}, u32[]{:S(2)}) collective-permute-start(bf16[128,1792]{1,0:T(8,128)(2,1)} %get-tuple-element.118), channel_id=1, source_target_pairs={{0,1},{1,2},{2,3},{3,0},{4,5},{5,6},{6,7},{7,4},{8,9},{9,10},{10,1... | collective-permute-start | bytes 1376264 | tf_op jit(solution)/shard_map/ppermute | solution.py:17
  736.6 39.9 %collective-permute-start.2 = (bf16[128,1792]{1,0:T(8,128)(2,1)}, bf16[128,1792]{1,0:T(8,128)(2,1)S(1)}, u32[]{:S(2)}, u32[]{:S(2)}) collective-permute-start(bf16[128,1792]{1,0:T(8,128)(2,1)} %get-tuple-element.118), channel_id=1, source_target_pairs={{0,3},{1,0},{2,1},{3,2},{4,7},{5,4},{6,5},{7,6},{8,11},{9,8},{10,9... | collective-permute-start | bytes 1376264 | tf_op jit(solution)/shard_map/ppermute | solution.py:20
  760.3 28.5 %collective-permute-start.1 = (bf16[128,1792]{1,0:T(8,128)(2,1)S(1)}, bf16[128,1792]{1,0:T(8,128)(2,1)S(1)}, u32[]{:S(2)}, u32[]{:S(2)}) collective-permute-start(bf16[128,1792]{1,0:T(8,128)(2,1)S(1)} %collective-permute-done), channel_id=1, source_target_pairs={{0,1},{1,2},{2,3},{3,0},{4,5},{5,6},{6,7},{7,4},{8,9},{9,10},{10,1... | collective-permute-start | bytes 1376264 | tf_op jit(solution)/shard_map/ppermute | solution.py:17
  822.5 165.6 %all-gather.33.cloned.1.call-start = ((), (), s32[]{:S(2)}) async-start(), calls=%async_computation.34 | async-start | bytes 2293760 | tf_op jit(solution)/shard_map/all_gather | solution.py:45
  923.9 151.9 %all-gather.41.cloned.1.call-start = ((), (), s32[]{:S(2)}) async-start(), calls=%async_computation.42 | async-start | bytes 2293760 | tf_op jit(solution)/shard_map/all_gather | solution.py:45
  923.9 18.2 collective-permute-start.6
  925.3 49.4 %collective-permute-start.8 = (bf16[128,1792]{1,0:T(8,128)(2,1)}, bf16[128,1792]{1,0:T(8,128)(2,1)S(1)}, u32[]{:S(2)}, u32[]{:S(2)}) collective-permute-start(bf16[128,1792]{1,0:T(8,128)(2,1)} %get-tuple-element.117), channel_id=1, source_target_pairs={{0,3},{1,0},{2,1},{3,2},{4,7},{5,4},{6,5},{7,6},{8,11},{9,8},{10,9... | collective-permute-start | bytes 1376264 | tf_op jit(solution)/shard_map/ppermute | solution.py:20
  942.1 38.0 %collective-permute-start.7 = (bf16[128,1792]{1,0:T(8,128)(2,1)S(1)}, bf16[128,1792]{1,0:T(8,128)(2,1)S(1)}, u32[]{:S(2)}, u32[]{:S(2)}) collective-permute-start(bf16[128,1792]{1,0:T(8,128)(2,1)S(1)} %collective-permute-done.6), channel_id=1, source_target_pairs={{0,1},{1,2},{2,3},{3,0},{4,5},{5,6},{6,7},{7,4},{8,9},{9,10},{10,1... | collective-permute-start | bytes 1376264 | tf_op jit(solution)/shard_map/ppermute | solution.py:17
  988.1 136.6 %reduce-scatter.48.cloned.1.call-start = ((), (), s32[]{:S(2)}) async-start(), calls=%async_computation.46 | async-start | bytes 4587520 | tf_op jit(solution)/shard_map/reduce_scatter | solution.py:57
  1013.9 180.2 %reduce-scatter.56.cloned.1.call-start = ((), (), s32[]{:S(2)}) async-start(), calls=%async_computation.50 | async-start | bytes 4587520 | tf_op jit(solution)/shard_map/reduce_scatter | solution.py:57
  1014.0 27.3 %collective-permute-start.18 = (bf16[128,1792]{1,0:T(8,128)(2,1)S(1)}, bf16[128,1792]{1,0:T(8,128)(2,1)S(1)}, u32[]{:S(2)}, u32[]{:S(2)}) collective-permute-start(bf16[128,1792]{1,0:T(8,128)(2,1)S(1)} %get-tuple-element.119), channel_id=1, source_target_pairs={{0,1},{1,2},{2,3},{3,0},{4,5},{5,6},{6,7},{7,4},{8,9},{9,10},{10,1... | collective-permute-start | bytes 1376264 | tf_op jit(solution)/shard_map/ppermute | solution.py:17
  1020.5 32.6 %collective-permute-start.20 = (bf16[128,1792]{1,0:T(8,128)(2,1)S(1)}, bf16[128,1792]{1,0:T(8,128)(2,1)S(1)}, u32[]{:S(2)}, u32[]{:S(2)}) collective-permute-start(bf16[128,1792]{1,0:T(8,128)(2,1)S(1)} %get-tuple-element.119), channel_id=1, source_target_pairs={{0,3},{1,0},{2,1},{3,2},{4,7},{5,4},{6,5},{7,6},{8,11},{9,8},{10,9... | collective-permute-start | bytes 1376264 | tf_op jit(solution)/shard_map/ppermute | solution.py:20
  1041.2 25.9 %collective-permute-start.19 = (bf16[128,1792]{1,0:T(8,128)(2,1)S(1)}, bf16[128,1792]{1,0:T(8,128)(2,1)S(1)}, u32[]{:S(2)}, u32[]{:S(2)}) collective-permute-start(bf16[128,1792]{1,0:T(8,128)(2,1)S(1)} %collective-permute-done.18), channel_id=1, source_target_pairs={{0,1},{1,2},{2,3},{3,0},{4,5},{5,6},{6,7},{7,4},{8,9},{9,10},{10,1... | collective-permute-start | bytes 1376264 | tf_op jit(solution)/shard_map/ppermute | solution.py:17
  1101.7 163.6 %reduce-scatter.34.cloned.1.call-start = ((), (), s32[]{:S(2)}) async-start(), calls=%async_computation.35 | async-start | bytes 4587520 | tf_op jit(solution)/shard_map/reduce_scatter | solution.py:53
  1109.0 227.3 %reduce-scatter.42.cloned.1.call-start = ((), (), s32[]{:S(2)}) async-start(), calls=%async_computation.43 | async-start | bytes 4587520 | tf_op jit(solution)/shard_map/reduce_scatter | solution.py:53
  1116.3 465.5 %all-reduce.22.cloned.1.call-start = ((), (), s32[]{:S(2)}) async-start(), calls=%async_computation.58 | async-start | bytes 524288
  1341.6 15.6 collective-permute-start.21
  1343.0 26.9 %collective-permute-start.23 = (bf16[128,1792]{1,0:T(8,128)(2,1)}, bf16[128,1792]{1,0:T(8,128)(2,1)}, u32[]{:S(2)}, u32[]{:S(2)}) collective-permute-start(bf16[128,1792]{1,0:T(8,128)(2,1)} %get-tuple-element.110), channel_id=1, source_target_pairs={{0,3},{1,0},{2,1},{3,2},{4,7},{5,4},{6,5},{7,6},{8,11},{9,8},{10,9... | collective-permute-start | bytes 1376264 | tf_op jit(solution)/shard_map/ppermute | solution.py:20
  1345.5 31.6 %collective-permute-start.15 = (bf16[128,1792]{1,0:T(8,128)(2,1)S(1)}, bf16[128,1792]{1,0:T(8,128)(2,1)}, u32[]{:S(2)}, u32[]{:S(2)}) collective-permute-start(bf16[128,1792]{1,0:T(8,128)(2,1)S(1)} %get-tuple-element.109), channel_id=1, source_target_pairs={{0,1},{1,2},{2,3},{3,0},{4,5},{5,6},{6,7},{7,4},{8,9},{9,10},{10,1... | collective-permute-start | bytes 1376264 | tf_op jit(solution)/shard_map/ppermute | solution.py:17
  1357.2 29.5 %collective-permute-start.22 = (bf16[128,1792]{1,0:T(8,128)(2,1)}, bf16[128,1792]{1,0:T(8,128)(2,1)}, u32[]{:S(2)}, u32[]{:S(2)}) collective-permute-start(bf16[128,1792]{1,0:T(8,128)(2,1)} %collective-permute-done.21), channel_id=1, source_target_pairs={{0,1},{1,2},{2,3},{3,0},{4,5},{5,6},{6,7},{7,4},{8,9},{9,10},{10,1... | collective-permute-start | bytes 1376264 | tf_op jit(solution)/shard_map/ppermute | solution.py:17
  1367.2 36.7 %collective-permute-start.17 = (bf16[128,1792]{1,0:T(8,128)(2,1)S(1)}, bf16[128,1792]{1,0:T(8,128)(2,1)S(1)}, u32[]{:S(2)}, u32[]{:S(2)}) collective-permute-start(bf16[128,1792]{1,0:T(8,128)(2,1)S(1)} %get-tuple-element.109), channel_id=1, source_target_pairs={{0,3},{1,0},{2,1},{3,2},{4,7},{5,4},{6,5},{7,6},{8,11},{9,8},{10,9... | collective-permute-start | bytes 1376264 | tf_op jit(solution)/shard_map/ppermute | solution.py:20
  1368.1 38.2 %collective-permute-start.3 = (bf16[128,1792]{1,0:T(8,128)(2,1)S(1)}, bf16[128,1792]{1,0:T(8,128)(2,1)S(1)}, u32[]{:S(2)}, u32[]{:S(2)}) collective-permute-start(bf16[128,1792]{1,0:T(8,128)(2,1)S(1)} %get-tuple-element.160), channel_id=1, source_target_pairs={{0,1},{1,2},{2,3},{3,0},{4,5},{5,6},{6,7},{7,4},{8,9},{9,10},{10,1... | collective-permute-start | bytes 1376264 | tf_op jit(solution)/shard_map/ppermute | solution.py:17
  1369.9 74.1 %collective-permute-start.5 = (bf16[128,1792]{1,0:T(8,128)(2,1)S(1)}, bf16[128,1792]{1,0:T(8,128)(2,1)S(1)}, u32[]{:S(2)}, u32[]{:S(2)}) collective-permute-start(bf16[128,1792]{1,0:T(8,128)(2,1)S(1)} %get-tuple-element.160), channel_id=1, source_target_pairs={{0,3},{1,0},{2,1},{3,2},{4,7},{5,4},{6,5},{7,6},{8,11},{9,8},{10,9... | collective-permute-start | bytes 1376264 | tf_op jit(solution)/shard_map/ppermute | solution.py:20
  1377.0 49.1 %collective-permute-start.9 = (bf16[128,1792]{1,0:T(8,128)(2,1)S(1)}, bf16[128,1792]{1,0:T(8,128)(2,1)S(1)}, u32[]{:S(2)}, u32[]{:S(2)}) collective-permute-start(bf16[128,1792]{1,0:T(8,128)(2,1)S(1)} %get-tuple-element.111), channel_id=1, source_target_pairs={{0,1},{1,2},{2,3},{3,0},{4,5},{5,6},{6,7},{7,4},{8,9},{9,10},{10,1... | collective-permute-start | bytes 1376264 | tf_op jit(solution)/shard_map/ppermute | solution.py:17
  1386.8 49.1 %collective-permute-start.16 = (bf16[128,1792]{1,0:T(8,128)(2,1)}, bf16[128,1792]{1,0:T(8,128)(2,1)S(1)}, u32[]{:S(2)}, u32[]{:S(2)}) collective-permute-start(bf16[128,1792]{1,0:T(8,128)(2,1)} %collective-permute-done.15), channel_id=1, source_target_pairs={{0,1},{1,2},{2,3},{3,0},{4,5},{5,6},{6,7},{7,4},{8,9},{9,10},{10,1... | collective-permute-start | bytes 1376264 | tf_op jit(solution)/shard_map/ppermute | solution.py:17
  1403.9 62.2 %collective-permute-start.11 = (bf16[128,1792]{1,0:T(8,128)(2,1)S(1)}, bf16[128,1792]{1,0:T(8,128)(2,1)S(1)}, u32[]{:S(2)}, u32[]{:S(2)}) collective-permute-start(bf16[128,1792]{1,0:T(8,128)(2,1)S(1)} %get-tuple-element.111), channel_id=1, source_target_pairs={{0,3},{1,0},{2,1},{3,2},{4,7},{5,4},{6,5},{7,6},{8,11},{9,8},{10,9... | collective-permute-start | bytes 1376264 | tf_op jit(solution)/shard_map/ppermute | solution.py:20
  1406.4 49.2 %collective-permute-start.4 = (bf16[128,1792]{1,0:T(8,128)(2,1)S(1)}, bf16[128,1792]{1,0:T(8,128)(2,1)S(1)}, u32[]{:S(2)}, u32[]{:S(2)}) collective-permute-start(bf16[128,1792]{1,0:T(8,128)(2,1)S(1)} %collective-permute-done.3), channel_id=1, source_target_pairs={{0,1},{1,2},{2,3},{3,0},{4,5},{5,6},{6,7},{7,4},{8,9},{9,10},{10,1... | collective-permute-start | bytes 1376264 | tf_op jit(solution)/shard_map/ppermute | solution.py:17
  1426.2 39.9 %collective-permute-start.10 = (bf16[128,1792]{1,0:T(8,128)(2,1)S(1)}, bf16[128,1792]{1,0:T(8,128)(2,1)S(1)}, u32[]{:S(2)}, u32[]{:S(2)}) collective-permute-start(bf16[128,1792]{1,0:T(8,128)(2,1)S(1)} %collective-permute-done.9), channel_id=1, source_target_pairs={{0,1},{1,2},{2,3},{3,0},{4,5},{5,6},{6,7},{7,4},{8,9},{9,10},{10,1... | collective-permute-start | bytes 1376264 | tf_op jit(solution)/shard_map/ppermute | solution.py:17
  1529.2 252.1 %reduce-scatter.54.cloned.1.call-start = ((), (), s32[]{:S(2)}) async-start(), calls=%async_computation.49 | async-start | bytes 4587520 | tf_op jit(solution)/shard_map/reduce_scatter | solution.py:57
  1589.6 191.7 %reduce-scatter.58.cloned.1.call-start = ((), (), s32[]{:S(2)}) async-start(), calls=%async_computation.51 | async-start | bytes 4587520 | tf_op jit(solution)/shard_map/reduce_scatter | solution.py:57
  1607.3 192.5 %reduce-scatter.50.cloned.1.call-start = ((), (), s32[]{:S(2)}) async-start(), calls=%async_computation.47 | async-start | bytes 4587520 | tf_op jit(solution)/shard_map/reduce_scatter | solution.py:57
  1624.7 246.3 %reduce-scatter.46.cloned.1.call-start = ((), (), s32[]{:S(2)}) async-start(), calls=%async_computation.45 | async-start | bytes 4587520 | tf_op jit(solution)/shard_map/reduce_scatter | solution.py:57
  1639.4 302.9 %reduce-scatter.38.cloned.1.call-start = ((), (), s32[]{:S(2)}) async-start(), calls=%async_computation.39 | async-start | bytes 4587520 | tf_op jit(solution)/shard_map/reduce_scatter | solution.py:53
  1647.5 366.0 %reduce-scatter.30.cloned.1.call-start = ((), (), s32[]{:S(2)}) async-start(), calls=%async_computation.31 | async-start | bytes 4587520 | tf_op jit(solution)/shard_map/reduce_scatter | solution.py:53
  1655.6 438.1 %reduce-scatter.66.cloned.1.call-start = ((), (), s32[]{:S(2)}) async-start(), calls=%async_computation.55 | async-start | bytes 10321920 | tf_op jit(solution)/shard_map/reduce_scatter | solution.py:218
  1686.4 486.4 %reduce-scatter.68.cloned.1.call-start = ((), (), s32[]{:S(2)}) async-start(), calls=%async_computation.56 | async-start | bytes 10321920 | tf_op jit(solution)/shard_map/reduce_scatter | solution.py:219
  1716.5 536.0 %reduce-scatter.70.cloned.1.call-start = ((), (), s32[]{:S(2)}) async-start(), calls=%async_computation.57 | async-start | bytes 10321920 | tf_op jit(solution)/shard_map/reduce_scatter | solution.py:220
  1748.3 557.0 %reduce-scatter.62.cloned.1.call-start = ((), (), s32[]{:S(2)}) async-start(), calls=%async_computation.53 | async-start | bytes 4128768 | tf_op jit(solution)/shard_map/reduce_scatter | solution.py:214
  1758.3 600.0 %reduce-scatter.64.cloned.1.call-start = ((), (), s32[]{:S(2)}) async-start(), calls=%async_computation.54 | async-start | bytes 4128768 | tf_op jit(solution)/shard_map/reduce_scatter | solution.py:216
  1768.5 642.4 %reduce-scatter.60.cloned.1.call-start = ((), (), s32[]{:S(2)}) async-start(), calls=%async_computation.52 | async-start | bytes 4128768 | tf_op jit(solution)/shard_map/reduce_scatter | solution.py:213
  (219 other events, 6377.5 us)
Sparse Core Ops, SparseCore 0:
  11.8 44.0 all-gather.14
  57.8 25.6 all-gather.16
  85.6 41.3 all-gather.30
  128.8 26.0 all-gather.18
  156.6 26.7 all-gather.20
  185.4 41.4 all-gather.34
  228.4 40.2 all-gather.38
  271.6 67.2 reduce-scatter.27
  341.2 68.7 reduce-scatter.35
  412.2 68.7 reduce-scatter.39
  483.3 68.7 reduce-scatter.31
  553.9 38.7 all-gather.24
  594.8 41.3 all-gather.36
  638.0 37.2 all-gather.26
  677.0 38.3 all-gather.28
  717.4 60.4 all-gather.22
  780.5 68.4 reduce-scatter.51
  851.2 68.2 reduce-scatter.43
  924.0 63.6 all-gather.32
  989.1 62.7 all-gather.40
  1054.7 69.9 reduce-scatter.47
  1127.0 67.0 reduce-scatter.55
  1196.4 68.7 reduce-scatter.33
  1267.4 68.7 reduce-scatter.41
  1529.3 52.4 all-reduce.21
  1589.7 67.7 reduce-scatter.53
  1659.8 68.7 reduce-scatter.57
  1731.0 68.7 reduce-scatter.49
  1802.2 68.7 reduce-scatter.45
  1873.3 69.0 reduce-scatter.37
  1944.8 68.7 reduce-scatter.29
  2018.2 75.4 reduce-scatter.65
  2097.7 75.0 reduce-scatter.67
  2177.5 75.0 reduce-scatter.69
  2256.6 48.6 reduce-scatter.61
  2309.6 48.6 reduce-scatter.63
  2362.2 48.7 reduce-scatter.59
